TPU v7x, 32 devices: a whole 2x2x4 slice. The times are simulated.
32 devices in a mesh: seq: 8 (over y, x, core), head: 4 (over z).
Axes of the slice: x: 2, y: 2, z: 4, core: 2. Of those that a mesh axis runs over, the one named last changes fastest.
Arguments:
- queries: bfloat16 [8192, 8192], P(('seq', 'head')), may hold values from -64 to 64
- key_rows: bfloat16 [8192, 1024], P(('seq', 'head')), may hold values from -6 to 6
- value_projection_rows: bfloat16 [8192, 1024], P(('seq', 'head')), may hold values from -6 to 6
- upstream: bfloat16 [8192, 8192], P(('seq', 'head')), may hold values from -6 to 6
- ancestors: int32 [128, 2], P('seq'), may hold values from -1 to 126, as said below
Outputs:
- attended: bfloat16 [8192, 8192], P(('seq', 'head'))
- query_grad: bfloat16 [8192, 8192], P(('seq', 'head'))
- key_grad: bfloat16 [8192, 1024], P(('seq', 'head'))
- value_grad: bfloat16 [8192, 1024], P(('seq', 'head'))
Inputs may be any that keep to these rules, and one draw needn't show every extreme that they name: `ancestors`: each entry of row b is -1 (no ancestor) or a block index from max(1, b - 32) to b - 1; where that range is not empty the first entry is b - 1, and where b is a multiple of 16 the last entry is the lowest index of that range. Entries of a row may repeat.
All inputs are finite; a program needn't handle non-finite values.
Results may differ from a plain program's by a relative error of at most 0.012.
The roundings to bfloat16 on the way count: a program that leaves them out, or rounds other values in their place, can miss the bound.
Values may be sent and summed in bfloat16 or wider, within the bound.
A program may use at most 192 MiB of HBM per device.

v0:
```python
import jax
import jax.numpy as jnp
from jax import lax
from jax.sharding import PartitionSpec as P

HEAD_SIZE = 128
MASK_BLOCK_SIZE = 64
ROOT = 64
ANC = 2
NEGATIVE = -1e30


def passed_along(x, axis, by):
    length = lax.axis_size(axis)
    pairs = [(i, i + by) for i in range(length) if 0 <= i + by < length]
    return lax.ppermute(x, axis, pairs)


def from_root(x, axis, root):
    mine = lax.axis_index(axis) == root
    return lax.psum(jnp.where(mine, x, jnp.zeros_like(x)), axis)


def block_scores(query_blocks, key_heads, shared):
    if shared:
        return jnp.einsum(
            "bqkgd,skd->bkgqs", query_blocks, key_heads, preferred_element_type=jnp.float32
        )
    return jnp.einsum(
        "bqkgd,bskd->bkgqs", query_blocks, key_heads, preferred_element_type=jnp.float32
    )


def block_apply(weights, rows_heads, shared):
    if shared:
        return jnp.einsum(
            "bkgqs,skd->bqkgd", weights, rows_heads, preferred_element_type=jnp.float32
        )
    return jnp.einsum("bkgqs,bskd->bqkgd", weights, rows_heads, preferred_element_type=jnp.float32)


def block_back(weights, query_side, shared):
    if shared:
        return jnp.einsum(
            "bkgqs,bqkgd->skd", weights, query_side, preferred_element_type=jnp.float32
        )
    return jnp.einsum("bkgqs,bqkgd->bskd", weights, query_side, preferred_element_type=jnp.float32)


def local(queries, key_rows, value_projection_rows, upstream, ancestors):
    local_query, local_key, local_value = (
        lax.all_to_all(queries, "head", split_axis=1, concat_axis=0, tiled=True),
        lax.all_to_all(key_rows, "head", split_axis=1, concat_axis=0, tiled=True),
        lax.all_to_all(value_projection_rows, "head", split_axis=1, concat_axis=0, tiled=True),
    )
    tokens = local_query.shape[0]
    nblocks = tokens // MASK_BLOCK_SIZE
    kv_width = local_key.shape[1]
    kv_heads = kv_width // HEAD_SIZE
    query_groups = local_query.shape[1] // HEAD_SIZE // kv_heads
    scale = HEAD_SIZE ** (-0.5)
    shard = lax.axis_index("seq")
    near_key, near_value = passed_along((local_key, local_value), "seq", 1)
    far_key, far_value = passed_along((local_key, local_value), "seq", 2)
    tree_root_key, tree_root_value = (
        from_root(local_key[:ROOT], "seq", 0),
        from_root(local_value[:ROOT], "seq", 0),
    )
    window_key = jnp.concatenate([far_key, near_key, local_key], 0).reshape(
        3 * nblocks, MASK_BLOCK_SIZE, kv_width
    )
    window_value = jnp.concatenate([far_value, near_value, local_value], 0).reshape(
        3 * nblocks, MASK_BLOCK_SIZE, kv_width
    )
    order = jnp.arange(ANC, dtype=jnp.int32)
    before = order[None, :] < order[:, None]
    repeated = jnp.any((ancestors[:, :, None] == ancestors[:, None, :]) & before[None], axis=2)
    valid = (ancestors >= 0) & jnp.logical_not(repeated)
    relative = jnp.clip(ancestors - (shard - 2) * nblocks, 0, 3 * nblocks - 1).reshape(-1)
    ancestor_key = jnp.take(window_key, relative, axis=0).reshape(
        nblocks, ANC * MASK_BLOCK_SIZE, kv_heads, HEAD_SIZE
    )
    ancestor_value = jnp.take(window_value, relative, axis=0).reshape(
        nblocks, ANC * MASK_BLOCK_SIZE, kv_heads, HEAD_SIZE
    )
    query_pos = (shard * tokens + jnp.arange(tokens, dtype=jnp.int32)).reshape(
        nblocks, MASK_BLOCK_SIZE
    )
    root_pos = jnp.arange(ROOT, dtype=jnp.int32)
    root_mask = root_pos[None, None, :] <= query_pos[:, :, None]
    own_mask = (query_pos[:, None, :] <= query_pos[:, :, None]) & (query_pos[:, None, :] >= ROOT)
    anc_mask = jnp.broadcast_to(
        jnp.repeat(valid, MASK_BLOCK_SIZE, axis=1)[:, None, :],
        (nblocks, MASK_BLOCK_SIZE, ANC * MASK_BLOCK_SIZE),
    )
    sections = [
        (
            tree_root_key.reshape(ROOT, kv_heads, HEAD_SIZE),
            tree_root_value.reshape(ROOT, kv_heads, HEAD_SIZE),
            root_mask,
            True,
        ),
        (
            local_key.reshape(nblocks, MASK_BLOCK_SIZE, kv_heads, HEAD_SIZE),
            local_value.reshape(nblocks, MASK_BLOCK_SIZE, kv_heads, HEAD_SIZE),
            own_mask,
            False,
        ),
        (ancestor_key, ancestor_value, anc_mask, False),
    ]
    query_blocks = local_query.reshape(nblocks, MASK_BLOCK_SIZE, kv_heads, query_groups, HEAD_SIZE)
    masked_list = []
    row_max = jnp.full((nblocks, kv_heads, query_groups, MASK_BLOCK_SIZE), NEGATIVE, jnp.float32)
    row_sum = jnp.zeros((nblocks, kv_heads, query_groups, MASK_BLOCK_SIZE), jnp.float32)
    for entry in sections:
        wide_mask = entry[2][:, None, None]
        masked = jnp.where(
            wide_mask, block_scores(query_blocks, entry[0], entry[3]) * scale, NEGATIVE
        )
        sect_max = jnp.max(masked, axis=-1)
        sect_sum = jnp.sum(
            jnp.where(wide_mask, jnp.exp(masked - sect_max[..., None]), 0.0), axis=-1
        )
        new_max = jnp.maximum(row_max, sect_max)
        row_sum = row_sum * jnp.exp(row_max - new_max) + sect_sum * jnp.exp(sect_max - new_max)
        row_max = new_max
        masked_list.append(masked)
    lse = (row_max + jnp.log(row_sum))[..., None]
    prob_list = []
    out_sum = jnp.zeros((nblocks, MASK_BLOCK_SIZE, kv_heads, query_groups, HEAD_SIZE), jnp.float32)
    for number in range(3):
        entry = sections[number]
        probs = jnp.where(entry[2][:, None, None], jnp.exp(masked_list[number] - lse), 0.0).astype(
            jnp.bfloat16
        )
        prob_list.append(probs)
        out_sum = out_sum + block_apply(probs, entry[1], entry[3])
    attended_heads = lax.optimization_barrier(out_sum.astype(jnp.bfloat16))
    attended = lax.all_to_all(
        attended_heads.reshape(tokens, -1), "head", split_axis=0, concat_axis=1, tiled=True
    )
    local_upstream = lax.all_to_all(upstream, "head", split_axis=1, concat_axis=0, tiled=True)
    upstream_blocks = local_upstream.reshape(
        nblocks, MASK_BLOCK_SIZE, kv_heads, query_groups, HEAD_SIZE
    )
    delta = jnp.sum(
        upstream_blocks.astype(jnp.float32) * attended_heads.astype(jnp.float32), axis=-1
    ).transpose(0, 2, 3, 1)[..., None]
    query_sum = jnp.zeros(
        (nblocks, MASK_BLOCK_SIZE, kv_heads, query_groups, HEAD_SIZE), jnp.float32
    )
    key_parts = []
    value_parts = []
    for number in range(3):
        entry = sections[number]
        probs = prob_list[number]
        dprob = block_scores(upstream_blocks, entry[1], entry[3])
        dscore = (probs.astype(jnp.float32) * (dprob - delta)).astype(jnp.bfloat16)
        query_sum = query_sum + block_apply(dscore, entry[0], entry[3])
        key_parts.append(scale * block_back(dscore, query_blocks, entry[3]))
        value_parts.append(block_back(probs, upstream_blocks, entry[3]))
    root_key_grad, root_value_grad = lax.psum(
        (key_parts[0].reshape(ROOT, kv_width), value_parts[0].reshape(ROOT, kv_width)), "seq"
    )
    own_key = key_parts[1].reshape(tokens, kv_width)
    own_value = value_parts[1].reshape(tokens, kv_width)
    anc_both = jnp.concatenate(
        [
            key_parts[2].reshape(nblocks * ANC, MASK_BLOCK_SIZE * kv_width),
            value_parts[2].reshape(nblocks * ANC, MASK_BLOCK_SIZE * kv_width),
        ],
        1,
    )
    placing = (jnp.arange(3 * nblocks, dtype=jnp.int32)[:, None] == relative[None, :]).astype(
        jnp.float32
    )
    window_both = jnp.dot(
        placing, anc_both, precision=lax.Precision.HIGHEST, preferred_element_type=jnp.float32
    )
    window_grad_key = window_both[:, : MASK_BLOCK_SIZE * kv_width].reshape(3 * tokens, kv_width)
    window_grad_value = window_both[:, MASK_BLOCK_SIZE * kv_width :].reshape(3 * tokens, kv_width)
    far_key_grad, far_value_grad = (window_grad_key[:tokens], window_grad_value[:tokens])
    near_key_grad, near_value_grad = (
        window_grad_key[tokens : 2 * tokens],
        window_grad_value[tokens : 2 * tokens],
    )
    self_key_grad, self_value_grad = (
        window_grad_key[2 * tokens :],
        window_grad_value[2 * tokens :],
    )
    one_key, one_value = passed_along((near_key_grad, near_value_grad), "seq", -1)
    two_key, two_value = (
        passed_along(far_key_grad.astype(jnp.bfloat16), "seq", -2).astype(far_key_grad.dtype),
        passed_along(far_value_grad.astype(jnp.bfloat16), "seq", -2).astype(far_value_grad.dtype),
    )
    back_key = one_key + two_key
    back_value = one_value + two_value
    first_shard = shard == 0
    root_key_full = jnp.zeros((tokens, kv_width), jnp.float32).at[:ROOT].set(root_key_grad)
    root_value_full = jnp.zeros((tokens, kv_width), jnp.float32).at[:ROOT].set(root_value_grad)
    key_total = own_key + self_key_grad + back_key + jnp.where(first_shard, root_key_full, 0.0)
    value_total = (
        own_value + self_value_grad + back_value + jnp.where(first_shard, root_value_full, 0.0)
    )
    query_local = (scale * query_sum).astype(jnp.bfloat16).reshape(tokens, -1)
    query_grad, key_grad, value_grad = (
        lax.all_to_all(query_local, "head", split_axis=0, concat_axis=1, tiled=True),
        lax.all_to_all(
            key_total.astype(jnp.bfloat16), "head", split_axis=0, concat_axis=1, tiled=True
        ),
        lax.all_to_all(
            value_total.astype(jnp.bfloat16), "head", split_axis=0, concat_axis=1, tiled=True
        ),
    )
    return (attended, query_grad, key_grad, value_grad)


def solution(mesh):
    placed = (
        P(("seq", "head"), None),
        P(("seq", "head"), None),
        P(("seq", "head"), None),
        P(("seq", "head"), None),
        P("seq", None),
    )
    return jax.shard_map(
        local,
        mesh=mesh,
        in_specs=placed,
        out_specs=(
            P(("seq", "head"), None),
            P(("seq", "head"), None),
            P(("seq", "head"), None),
            P(("seq", "head"), None),
        ),
        check_vma=False,
    )
```

profile of v0, /device:TPU:0, one launch (start us, length us, event | category | flops | bytes accessed | tf_op | source)
XLA Modules:
  0.0 652.3 jit_solution(6052750993636207971)
XLA Ops:
  9.0 6.3 all-to-all-start.1
  17.2 12.6 %all-to-all-done.1 = bf16[256,4,256]{2,0,1:T(8,128)(2,1)S(1)} async-done(((bf16[256,4,256]{2,0,1:T(8,128)(2,1)}), bf16[256,4,256]{2,0,1:T(8,128)(2,1)S(1)}, u32[]{:S(2)}, u32[]{:S(2)}) %all-to-all-start.1) | async-done | bytes 524320 | tf_op jit(solution)/shard_map/all_to_all | solution.py:53
  29.8 3.5 all-to-all-start
  33.3 4.8 copy.506
  38.1 9.2 %all-to-all-done = bf16[256,4,256]{2,0,1:T(8,128)(2,1)S(1)} async-done(((bf16[256,4,256]{2,0,1:T(8,128)(2,1)}), bf16[256,4,256]{2,0,1:T(8,128)(2,1)S(1)}, u32[]{:S(2)}, u32[]{:S(2)}) %all-to-all-start) | async-done | bytes 524320 | tf_op jit(solution)/shard_map/all_to_all | solution.py:54
  47.3 5.0 all-to-all-start.2
  52.9 4.7 copy.505
  58.7 3.4 collective-permute-start
  62.2 2.1 collective-permute-start.1
  64.3 4.0 collective-permute-start.2
  68.3 4.0 collective-permute-start.3
  78.4 7.6 %collective-permute-done.2 = bf16[1024,256]{1,0:T(8,128)(2,1)} collective-permute-done((bf16[1024,256]{1,0:T(8,128)(2,1)S(1)}, bf16[1024,256]{1,0:T(8,128)(2,1)}, u32[]{:S(2)}, u32[]{:S(2)}) %collective-permute-start.2) | collective-permute-done | bytes 524320 | tf_op jit(solution)/shard_map/ppermute | solution.py:16
  92.9 52.1 %all-to-all-done.2 = bf16[256,4,2048]{2,0,1:T(8,128)(2,1)} async-done(((bf16[256,4,2048]{2,0,1:T(8,128)(2,1)}), bf16[256,4,2048]{2,0,1:T(8,128)(2,1)}, u32[]{:S(2)}, u32[]{:S(2)}) %all-to-all-start.2) | async-done | bytes 4194336 | tf_op jit(solution)/shard_map/all_to_all | solution.py:52
  145.0 4.8 all-to-all-start.4
  149.9 5.7 copy.384
  155.6 8.5 %bitcast_reduce_fusion = (f32[16,2,8,64]{3,2,1,0:T(8,128)}, f32[16,2,128,64,8]{2,3,4,1,0:T(8,128)}) fusion(pred[16,128]{1,0:T(8,128)(4,1)S(1)} %broadcast_in_dim_reshape.2, bf16[16,64,2,8,128]{4,3,2,1,0:T(8,128)(2,1)} %bitcast.91, bf16[16,128,2,128,1]{3,2,1,0,4:T(2,128)(2,1)S(1)} %bitcast.263), kind=kOutput, calls=%fused_computation.20 | convolution fusion | flops 543145984 | bytes 13699072 | tf_op jit(solution)/shard_map/bqkgd,bskd->bkgqs/dot_general | solution.py:29
  164.1 6.4 fusion.15
  170.5 2.9 select_reduce_fusion.1
  173.4 6.1 fusion.16
  179.6 2.9 select_reduce_fusion
  182.5 4.7 fusion.11
  187.4 4.2 select_convert_fusion
  191.7 5.5 fusion.127
  197.1 5.1 fusion.14
  202.3 4.6 fusion.31
  206.9 9.6 %fusion.8 = bf16[16,64,2,8,128]{4,1,3,0,2:T(8,128)(2,1)} fusion(f32[16,2,128,8,64]{2,4,3,0,1:T(8,128)} %fusion.31, f32[2,128,16,8,64]{1,4,3,2,0:T(8,128)} %fusion.127, bf16[16,2,8,64,64]{3,4,2,0,1:T(8,128)(2,1)S(1)} %get-tuple-element.55, bf16[16,64,2,128,1]{3,2,1,0,4:T(2,128)(2,1)S(1)} %bitcast.255), kind=kOutput, calls=%fused_computation.16 | convolution fusion | flops 274726912 | bytes 23592960 | tf_op jit(solution)/shard_map/bkgqs,bskd->bqkgd/dot_general | solution.py:39
  216.5 26.0 %all-to-all-done.4 = bf16[256,4,2048]{2,0,1:T(8,128)(2,1)} async-done(((bf16[256,4,2048]{2,0,1:T(8,128)(2,1)}), bf16[256,4,2048]{2,0,1:T(8,128)(2,1)}, u32[]{:S(2)}, u32[]{:S(2)}) %all-to-all-start.4) | async-done | bytes 4194336 | tf_op jit(solution)/shard_map/all_to_all | solution.py:142
  242.5 3.7 copy.385
  246.3 3.3 fusion.53
  250.7 2.4 multiply_reduce_fusion
  253.2 6.7 %fusion.3 = bf16[16,2,8,64,128]{4,3,2,1,0:T(8,128)(2,1)} fusion(bf16[16,2,8,64,128]{4,3,2,1,0:T(8,128)(2,1)} %copy-done.6, bf16[16,64,2,8,128]{4,3,2,1,0:T(8,128)(2,1)S(1)} %bitcast.230, bf16[16,128,2,128,1]{3,2,1,0,4:T(2,128)(2,1)S(1)} %bitcast.242, f32[16,64,2,8]{1,3,0,2:T(8,128)S(1)} %multiply_reduce_fusion), kind=kOutput, calls=%fused_computation.7 | convolution fusion | flops 545259520 | bytes 13697024 | tf_op jit(solution)/shard_map/bqkgd,bskd->bkgqs/dot_general | solution.py:29
  259.9 7.8 %fusion.5 = bf16[16,2,8,64,64]{3,4,2,0,1:T(8,128)(2,1)} fusion(bf16[16,2,8,64,64]{3,4,2,0,1:T(8,128)(2,1)} %copy-done.3, f32[16,2,8,64]{3,2,0,1:T(8,128)S(1)} %bitcast.265, bf16[16,64,2,8,128]{4,3,2,1,0:T(8,128)(2,1)S(1)} %bitcast.231, bf16[16,64,2,128,1]{3,2,1,0,4:T(2,128)(2,1)S(1)} %bitcast.256), kind=kOutput, calls=%fused_computation.11 | convolution fusion | flops 272629760 | bytes 8978432 | tf_op jit(solution)/shard_map/bqkgd,bskd->bkgqs/dot_general | solution.py:29
  267.7 5.6 fusion.7
  273.3 2.6 fusion.61
  275.9 4.2 fusion.50
  281.7 2.7 reshape.256
  284.5 3.2 copy.321
  287.7 2.8 reshape.257
  290.6 5.1 fusion.136
  297.7 2.4 slice.87
  306.0 6.1 fusion.71
  314.6 5.1 fusion.91
  322.1 5.1 fusion.81
  327.4 3.1 copy.317
  331.9 3.0 copy.328
  337.0 13.6 %collective-permute-done.7 = bf16[1024,256]{1,0:T(8,128)(2,1)} collective-permute-done((bf16[1024,256]{1,0:T(8,128)(2,1)}, bf16[1024,256]{1,0:T(8,128)(2,1)}, u32[]{:S(2)}, u32[]{:S(2)}) %collective-permute-start.7) | collective-permute-done | bytes 524320 | tf_op jit(solution)/shard_map/ppermute | solution.py:16
  352.2 40.7 %all-reduce.5.cloned.1.call-done = (f32[64,256]{1,0:T(8,128)}, f32[64,256]{1,0:T(8,128)}) async-done(((f32[64,256]{1,0:T(8,128)}, f32[64,256]{1,0:T(8,128)}), (f32[64,256]{1,0:T(8,128)}, f32[64,256]{1,0:T(8,128)})) %all-reduce.5.cloned.1.call-update) | async-done | bytes 131088 | tf_op jit(solution)/shard_map/psum | solution.py:162
  394.7 4.6 all-to-all-start.6
  399.3 7.4 %fusion.129 = f32[2,128,16,8,64]{1,4,3,2,0:T(8,128)} fusion(bf16[16,2,8,64,64]{3,4,2,0,1:T(8,128)(2,1)} %fusion.7, bf16[64,2,128]{2,0,1:T(8,128)(2,1)S(1)} %copy-done.28), kind=kOutput, calls=%fused_computation.140 | convolution fusion | flops 268435456 | bytes 10518528 | tf_op jit(solution)/shard_map/bkgqs,skd->bqkgd/dot_general | solution.py:36
  406.7 4.5 fusion.29
  412.2 5.2 all-to-all-start.7
  417.3 9.0 %fusion.1 = bf16[16,64,2,8,128]{4,1,3,0,2:T(8,128)(2,1)S(1)} fusion(f32[16,2,128,8,64]{2,4,3,0,1:T(8,128)} %fusion.29, f32[2,128,16,8,64]{1,4,3,2,0:T(8,128)} %fusion.129, bf16[16,2,8,64,64]{3,4,2,0,1:T(8,128)(2,1)} %fusion.5, bf16[16,64,2,128,1]{3,2,1,0,4:T(2,128)(2,1)S(1)} %bitcast.254), kind=kOutput, calls=%fused_computation.4 | convolution fusion | flops 276824064 | bytes 23592960 | tf_op jit(solution)/shard_map/bkgqs,bskd->bqkgd/dot_general | solution.py:39
  426.4 5.6 copy.313
  432.0 7.3 %all_to_all.126 = bf16[4,256,2048]{2,1,0:T(8,128)(2,1)} reshape(bf16[16,64,2,8,128]{4,3,2,1,0:T(8,128)(2,1)} %copy.313) | data formatting | bytes 8388608 | tf_op jit(solution)/shard_map/all_to_all | solution.py:207
  439.3 5.1 all-to-all-start.5
  444.4 7.7 %copy.298 = bf16[16,64,2,8,128]{4,3,2,1,0:T(8,128)(2,1)} copy(bf16[16,64,2,8,128]{4,1,3,0,2:T(8,128)(2,1)} %fusion.8) | data formatting | bytes 8388608 | tf_op jit(solution)/shard_map/optimization_barrier | solution.py:138
  452.1 7.3 %all_to_all.119 = bf16[4,256,2048]{2,1,0:T(8,128)(2,1)} reshape(bf16[16,64,2,8,128]{4,3,2,1,0:T(8,128)(2,1)} %copy.298) | data formatting | bytes 8388608 | tf_op jit(solution)/shard_map/all_to_all | solution.py:139
  459.4 75.8 %all-to-all-done.5 = bf16[4,256,2048]{2,1,0:T(8,128)(2,1)} async-done(((bf16[4,256,2048]{2,1,0:T(8,128)(2,1)}), bf16[4,256,2048]{2,1,0:T(8,128)(2,1)}, u32[]{:S(2)}, u32[]{:S(2)}) %all-to-all-start.5) | async-done | bytes 4194336 | tf_op jit(solution)/shard_map/all_to_all | solution.py:207
  535.2 4.9 all-to-all-start.3
  541.8 6.2 copy.314
  548.0 6.3 copy.334
  554.3 78.4 %all-to-all-done.3 = bf16[4,256,2048]{2,1,0:T(8,128)(2,1)} async-done(((bf16[4,256,2048]{2,1,0:T(8,128)(2,1)}), bf16[4,256,2048]{2,1,0:T(8,128)(2,1)}, u32[]{:S(2)}, u32[]{:S(2)}) %all-to-all-start.3) | async-done | bytes 4194336 | tf_op jit(solution)/shard_map/all_to_all | solution.py:139
  632.7 6.2 copy.299
  638.9 6.3 copy.333
  (130 shorter events, 44.0 us)
Async XLA Ops:
  9.0 20.8 %all-to-all-start.1 = ((bf16[256,4,256]{2,0,1:T(8,128)(2,1)}), bf16[256,4,256]{2,0,1:T(8,128)(2,1)S(1)}, u32[]{:S(2)}, u32[]{:S(2)}) async-start(bf16[256,4,256]{2,0,1:T(8,128)(2,1)} %bitcast.224), calls=%async_computation.1 | async-start | bytes 1048576 | tf_op jit(solution)/shard_map/all_to_all | solution.py:53
  29.8 17.4 %all-to-all-start = ((bf16[256,4,256]{2,0,1:T(8,128)(2,1)}), bf16[256,4,256]{2,0,1:T(8,128)(2,1)S(1)}, u32[]{:S(2)}, u32[]{:S(2)}) async-start(bf16[256,4,256]{2,0,1:T(8,128)(2,1)} %bitcast.225), calls=%async_computation | async-start | bytes 1048576 | tf_op jit(solution)/shard_map/all_to_all | solution.py:54
  47.3 5.1 copy-start.30
  47.3 97.7 %all-to-all-start.2 = ((bf16[256,4,2048]{2,0,1:T(8,128)(2,1)}), bf16[256,4,2048]{2,0,1:T(8,128)(2,1)}, u32[]{:S(2)}, u32[]{:S(2)}) async-start(bf16[256,4,2048]{2,0,1:T(8,128)(2,1)} %bitcast.238), calls=%async_computation.2 | async-start | bytes 8388608 | tf_op jit(solution)/shard_map/all_to_all | solution.py:52
  52.3 111.8 %all-reduce.7.cloned.1.call-start = ((), (), s32[]{:S(2)}) async-start(), calls=%async_computation.9 | async-start | bytes 131072 | tf_op jit(solution)/shard_map/psum | solution.py:21
  58.7 111.8 %copy-start.23 = (pred[16,64,64]{1,2,0:T(8,128)(4,1)}, pred[16,64,64]{1,2,0:T(8,128)(4,1)S(1)}, u32[]{:S(2)}) copy-start(pred[16,64,64]{1,2,0:T(8,128)(4,1)S(1)} %get-tuple-element.58) | copy-start | bytes 196612
  58.7 15.9 %collective-permute-start = (bf16[1024,256]{1,0:T(8,128)(2,1)S(1)}, bf16[1024,256]{1,0:T(8,128)(2,1)S(1)}, u32[]{:S(2)}, u32[]{:S(2)}) collective-permute-start(bf16[1024,256]{1,0:T(8,128)(2,1)S(1)} %bitcast.248), channel_id=1, source_target_pairs={{0,8},{4,12},{8,16},{12,20},{16,24},{20,28},{1,9},{5,13},{9,17},{1... | collective-permute-start | bytes 1572872 | tf_op jit(solution)/shard_map/ppermute | solution.py:16
  62.2 13.3 %collective-permute-start.1 = (bf16[1024,256]{1,0:T(8,128)(2,1)S(1)}, bf16[1024,256]{1,0:T(8,128)(2,1)}, u32[]{:S(2)}, u32[]{:S(2)}) collective-permute-start(bf16[1024,256]{1,0:T(8,128)(2,1)S(1)} %bitcast.249), channel_id=1, source_target_pairs={{0,4},{4,8},{8,12},{12,16},{16,20},{20,24},{24,28},{1,5},{5,9},{9,... | collective-permute-start | bytes 1572872 | tf_op jit(solution)/shard_map/ppermute | solution.py:16
  64.3 21.7 %collective-permute-start.2 = (bf16[1024,256]{1,0:T(8,128)(2,1)S(1)}, bf16[1024,256]{1,0:T(8,128)(2,1)}, u32[]{:S(2)}, u32[]{:S(2)}) collective-permute-start(bf16[1024,256]{1,0:T(8,128)(2,1)S(1)} %bitcast.243), channel_id=1, source_target_pairs={{0,8},{4,12},{8,16},{12,20},{16,24},{20,28},{1,9},{5,13},{9,17},{1... | collective-permute-start | bytes 1572872 | tf_op jit(solution)/shard_map/ppermute | solution.py:16
  68.3 17.7 %collective-permute-start.3 = (bf16[1024,256]{1,0:T(8,128)(2,1)S(1)}, bf16[1024,256]{1,0:T(8,128)(2,1)}, u32[]{:S(2)}, u32[]{:S(2)}) collective-permute-start(bf16[1024,256]{1,0:T(8,128)(2,1)S(1)} %bitcast.244), channel_id=1, source_target_pairs={{0,4},{4,8},{8,12},{12,16},{16,20},{20,24},{24,28},{1,5},{5,9},{9,... | collective-permute-start | bytes 1572872 | tf_op jit(solution)/shard_map/ppermute | solution.py:16
  72.4 101.0 %copy-start.12 = (bf16[16,64,2,128]{3,2,1,0:T(2,128)(2,1)}, bf16[16,64,2,128]{3,2,1,0:T(2,128)(2,1)S(1)}, u32[]{:S(2)}) copy-start(bf16[16,64,2,128]{3,2,1,0:T(2,128)(2,1)S(1)} %reshape.247) | copy-start | bytes 1572868
  74.7 0.8 copy-start.27
  145.0 97.5 %all-to-all-start.4 = ((bf16[256,4,2048]{2,0,1:T(8,128)(2,1)}), bf16[256,4,2048]{2,0,1:T(8,128)(2,1)}, u32[]{:S(2)}, u32[]{:S(2)}) async-start(bf16[256,4,2048]{2,0,1:T(8,128)(2,1)} %bitcast.237), calls=%async_computation.4 | async-start | bytes 8388608 | tf_op jit(solution)/shard_map/all_to_all | solution.py:142
  149.8 243.1 %all-reduce.5.cloned.1.call-start = ((), (), s32[]{:S(2)}) async-start(), calls=%async_computation.8 | async-start | bytes 262144 | tf_op jit(solution)/shard_map/psum | solution.py:162
  149.9 5.7 copy-start.16
  170.5 2.9 copy-start.21
  170.5 11.9 %slice-start = ((s8[8388608]{0:T(1024)(128)(4,1)}), s8[4194304]{0:T(1024)(128)(4,1)S(1)}, s32[]{:S(2)}) async-start(s8[8388608]{0:T(1024)(128)(4,1)} %bitcast.235), calls=%async_computation.10 | async-start | bytes 8388608
  173.4 9.0 %slice-start.1 = ((s8[8388608]{0:T(1024)(128)(4,1)}), s8[4194304]{0:T(1024)(128)(4,1)S(1)}, s32[]{:S(2)}) async-start(s8[8388608]{0:T(1024)(128)(4,1)} %bitcast.235), calls=%async_computation.11 | async-start | bytes 8388608
  179.5 2.9 copy-start.26
  182.5 4.9 copy-start.22
  182.5 4.9 copy-start.24
  187.4 4.3 copy-start.29
  191.6 5.5 copy-start.1
  191.7 15.2 %copy-start.3 = (bf16[16,2,8,64,64]{3,4,2,0,1:T(8,128)(2,1)}, bf16[16,2,8,64,64]{3,4,2,0,1:T(8,128)(2,1)S(1)}, u32[]{:S(2)}) copy-start(bf16[16,2,8,64,64]{3,4,2,0,1:T(8,128)(2,1)S(1)} %get-tuple-element.55) | copy-start | bytes 6291460
  197.1 5.1 copy-start.10
  202.2 4.6 copy-start.6
  202.3 4.6 copy-start.14
  242.5 3.8 copy-start.7
  246.3 27.1 %copy-start = (bf16[128,8,16,128]{3,2,1,0:T(8,128)(2,1)}, bf16[128,8,16,128]{3,2,1,0:T(8,128)(2,1)S(1)}, u32[]{:S(2)}) copy-start(bf16[128,8,16,128]{3,2,1,0:T(8,128)(2,1)S(1)} %copy.385) | copy-start | bytes 12582916
  246.3 4.5 copy-start.5
  250.7 2.4 copy-start.11
  259.9 7.8 %copy-start.2 = (bf16[16,2,8,64,64]{3,4,2,0,1:T(8,128)(2,1)S(1)}, bf16[16,2,8,64,64]{3,4,2,0,1:T(8,128)(2,1)}, u32[]{:S(2)}) copy-start(bf16[16,2,8,64,64]{3,4,2,0,1:T(8,128)(2,1)} %copy-done.1) | copy-start | bytes 6291460
  267.7 5.6 copy-start.4
  273.3 2.6 copy-start.8
  300.1 34.9 %collective-permute-start.4 = (f32[1024,256]{1,0:T(8,128)}, f32[1024,256]{1,0:T(8,128)}, u32[]{:S(2)}, u32[]{:S(2)}) collective-permute-start(f32[1024,256]{1,0:T(8,128)} %slice.87), channel_id=1, source_target_pairs={{4,0},{8,4},{12,8},{16,12},{20,16},{24,20},{28,24},{5,1},{9,5},{13... | collective-permute-start | bytes 3145736 | tf_op jit(solution)/shard_map/ppermute | solution.py:16
  304.5 7.5 %copy-start.20 = (f32[16,16384]{1,0:T(8,128)S(1)}, f32[16,16384]{1,0:T(8,128)}, u32[]{:S(2)}) copy-start(f32[16,16384]{1,0:T(8,128)} %get-tuple-element.49) | copy-start | bytes 3145732
  304.5 30.4 %collective-permute-start.5 = (bf16[1024,256]{1,0:T(8,128)(2,1)}, bf16[1024,256]{1,0:T(8,128)(2,1)}, u32[]{:S(2)}, u32[]{:S(2)}) collective-permute-start(bf16[1024,256]{1,0:T(8,128)(2,1)} %convert_element_type.73), channel_id=1, source_target_pairs={{8,0},{12,4},{16,8},{20,12},{24,16},{28,20},{9,1},{13,5},{17,9},{2... | collective-permute-start | bytes 1572872 | tf_op jit(solution)/shard_map/ppermute | solution.py:16
  313.2 6.5 copy-start.25
  313.2 37.4 %collective-permute-start.6 = (f32[1024,256]{1,0:T(8,128)}, f32[1024,256]{1,0:T(8,128)}, u32[]{:S(2)}, u32[]{:S(2)}) collective-permute-start(f32[1024,256]{1,0:T(8,128)} %slice.92), channel_id=1, source_target_pairs={{4,0},{8,4},{12,8},{16,12},{20,16},{24,20},{28,24},{5,1},{9,5},{13... | collective-permute-start | bytes 3145736 | tf_op jit(solution)/shard_map/ppermute | solution.py:16
  320.7 6.5 copy-start.19
  320.7 29.9 %collective-permute-start.7 = (bf16[1024,256]{1,0:T(8,128)(2,1)}, bf16[1024,256]{1,0:T(8,128)(2,1)}, u32[]{:S(2)}, u32[]{:S(2)}) collective-permute-start(bf16[1024,256]{1,0:T(8,128)(2,1)} %convert_element_type.76), channel_id=1, source_target_pairs={{8,0},{12,4},{16,8},{20,12},{24,16},{28,20},{9,1},{13,5},{17,9},{2... | collective-permute-start | bytes 1572872 | tf_op jit(solution)/shard_map/ppermute | solution.py:16
  327.2 4.6 copy-start.18
  335.0 15.6 %copy-start.15 = (f32[16,64,2,128]{3,2,1,0:T(2,128)S(1)}, f32[16,64,2,128]{3,2,1,0:T(2,128)}, u32[]{:S(2)}) copy-start(f32[16,64,2,128]{3,2,1,0:T(2,128)} %copy.328) | copy-start | bytes 3145732
  337.0 62.3 %copy-start.28 = (bf16[64,2,128]{2,0,1:T(8,128)(2,1)S(1)}, bf16[64,2,128]{2,0,1:T(8,128)(2,1)}, u32[]{:S(2)}) copy-start(bf16[64,2,128]{2,0,1:T(8,128)(2,1)} %get-tuple-element.47) | copy-start | bytes 98308
  394.7 17.5 %all-to-all-start.6 = ((bf16[4,256,256]{2,1,0:T(8,128)(2,1)}), bf16[4,256,256]{2,1,0:T(8,128)(2,1)S(1)}, u32[]{:S(2)}, u32[]{:S(2)}) async-start(bf16[4,256,256]{2,1,0:T(8,128)(2,1)} %bitcast.53), calls=%async_computation.6 | async-start | bytes 1048576 | tf_op jit(solution)/shard_map/all_to_all | solution.py:208
  399.3 7.4 %copy-start.9 = (bf16[16,2,8,64,128]{4,3,2,1,0:T(8,128)(2,1)S(1)}, bf16[16,2,8,64,128]{4,3,2,1,0:T(8,128)(2,1)}, u32[]{:S(2)}) copy-start(bf16[16,2,8,64,128]{4,3,2,1,0:T(8,128)(2,1)} %fusion.3) | copy-start | bytes 12582916
  399.3 7.4 %copy-start.17 = (bf16[16,128,2,128]{3,2,1,0:T(2,128)(2,1)S(1)}, bf16[16,128,2,128]{3,2,1,0:T(2,128)(2,1)}, u32[]{:S(2)}) copy-start(bf16[16,128,2,128]{3,2,1,0:T(2,128)(2,1)} %reshape.250) | copy-start | bytes 3145732
  406.7 10.7 %copy-start.13 = (bf16[16,64,2,128]{3,2,1,0:T(2,128)(2,1)S(1)}, bf16[16,64,2,128]{3,2,1,0:T(2,128)(2,1)}, u32[]{:S(2)}) copy-start(bf16[16,64,2,128]{3,2,1,0:T(2,128)(2,1)} %copy-done.12) | copy-start | bytes 1572868
  412.2 27.1 %all-to-all-start.7 = ((bf16[4,256,256]{2,1,0:T(8,128)(2,1)}), bf16[4,256,256]{2,1,0:T(8,128)(2,1)S(1)}, u32[]{:S(2)}, u32[]{:S(2)}) async-start(bf16[4,256,256]{2,1,0:T(8,128)(2,1)} %bitcast.61), calls=%async_computation.7 | async-start | bytes 1048576 | tf_op jit(solution)/shard_map/all_to_all | solution.py:211
  439.3 95.9 %all-to-all-start.5 = ((bf16[4,256,2048]{2,1,0:T(8,128)(2,1)}), bf16[4,256,2048]{2,1,0:T(8,128)(2,1)}, u32[]{:S(2)}, u32[]{:S(2)}) async-start(bf16[4,256,2048]{2,1,0:T(8,128)(2,1)} %all_to_all.126), calls=%async_computation.5 | async-start | bytes 8388608 | tf_op jit(solution)/shard_map/all_to_all | solution.py:207
  535.2 97.5 %all-to-all-start.3 = ((bf16[4,256,2048]{2,1,0:T(8,128)(2,1)}), bf16[4,256,2048]{2,1,0:T(8,128)(2,1)}, u32[]{:S(2)}, u32[]{:S(2)}) async-start(bf16[4,256,2048]{2,1,0:T(8,128)(2,1)} %all_to_all.119), calls=%async_computation.3 | async-start | bytes 8388608 | tf_op jit(solution)/shard_map/all_to_all | solution.py:139
Sparse Core Ops, SparseCore 0:
  74.8 52.4 all-reduce.6
  335.1 57.8 all-reduce.4
where the time goes:
time: 660 us; the launch traced here: 652 us
  waiting for transfers between devices  316 us (48%)
  local copies, waits for them, and re-layouts  114 us (17%)
  matrix products  113 us (17%)
  starting transfers between devices  58.5 us (9%)
  other arithmetic  35.4 us (5%)
  between operations  14.9 us (2%)
    all_to_all x1, waiting for transfers between devices, local(): lax.all_to_all(attended_heads.reshape(tokens, -1), 'head', split_axis=0,...  78.4 us
    all_to_all x1, waiting for transfers between devices, local(): lax.all_to_all(query_local, 'head', split_axis=0, concat_axis=1, tiled=True)  75.8 us
    all_to_all x1, waiting for transfers between devices, local(): lax.all_to_all(queries, 'head', split_axis=1, concat_axis=0, tiled=True)  52.1 us
    psum x1, waiting for transfers between devices, local(): lax.psum((key_parts[0].reshape(ROOT, kv_width), value_parts[0].reshape(RO...  40.7 us
    dot_general x4, matrix products, block_scores(): jnp.einsum('bqkgd,bskd->bkgqs', query_blocks, key_heads, preferred_elemen...  29.1 us
    dot_general x4, matrix products, block_apply(): jnp.einsum('bkgqs,bskd->bqkgd', weights, rows_heads, preferred_element_ty...  27.7 us
    all_to_all x1, waiting for transfers between devices, local(): lax.all_to_all(upstream, 'head', split_axis=1, concat_axis=0, tiled=True)  26 us
    unnamed x70, local copies, waits for them, and re-layouts  24.1 us
  transfers between devices with their start and end apart: 18, of which 10 were waited for; matrix products, arithmetic and copies ran while one was open for 27% of the time, Pallas kernels for 0%

commit v1 on v0

--- a/solution.py
+++ b/solution.py
@@ -50,7 +50,12 @@
 def local(queries, key_rows, value_projection_rows, upstream, ancestors):
     local_query, local_key, local_value = (
         lax.all_to_all(queries, "head", split_axis=1, concat_axis=0, tiled=True),
-        lax.all_to_all(key_rows, "head", split_axis=1, concat_axis=0, tiled=True),
+        jnp.concatenate(
+            lax.all_to_all(
+                jnp.stack(jnp.split(key_rows, lax.axis_size("head"), axis=1)), "head", 0, 0
+            ),
+            axis=0,
+        ),
         lax.all_to_all(value_projection_rows, "head", split_axis=1, concat_axis=0, tiled=True),
     )
     tokens = local_query.shape[0]

time: 660 us -> 660 us (level)
  no operation moved by 1% of the time
where the time goes in v1:
time: 660 us; the launch traced here: 653 us
  waiting for transfers between devices  316 us (48%)
  local copies, waits for them, and re-layouts  114 us (17%)
  matrix products  113 us (17%)
  starting transfers between devices  58.5 us (9%)
  other arithmetic  36.3 us (5%)
  between operations  14.9 us (2%)
    all_to_all x1, waiting for transfers between devices, local(): lax.all_to_all(attended_heads.reshape(tokens, -1), 'head', split_axis=0,...  78.4 us
    all_to_all x1, waiting for transfers between devices, local(): lax.all_to_all(query_local, 'head', split_axis=0, concat_axis=1, tiled=True)  75.8 us
    all_to_all x1, waiting for transfers between devices, local(): lax.all_to_all(queries, 'head', split_axis=1, concat_axis=0, tiled=True)  52.1 us
    psum x1, waiting for transfers between devices, local(): lax.psum((key_parts[0].reshape(ROOT, kv_width), value_parts[0].reshape(RO...  40.7 us
    dot_general x4, matrix products, block_scores(): jnp.einsum('bqkgd,bskd->bkgqs', query_blocks, key_heads, preferred_elemen...  29.1 us
    dot_general x4, matrix products, block_apply(): jnp.einsum('bkgqs,bskd->bqkgd', weights, rows_heads, preferred_element_ty...  27.7 us
    all_to_all x1, waiting for transfers between devices, local(): lax.all_to_all(upstream, 'head', split_axis=1, concat_axis=0, tiled=True)  26 us
    unnamed x70, local copies, waits for them, and re-layouts  24.2 us
  transfers between devices with their start and end apart: 18, of which 10 were waited for; matrix products, arithmetic and copies ran while one was open for 27% of the time, Pallas kernels for 0%

profile of v1, /device:TPU:0, one launch (start us, length us, event | category | flops | bytes accessed | tf_op | source)
XLA Modules:
  0.0 652.5 jit_solution(18167614072458790293)
XLA Ops:
  9.2 6.3 all-to-all-start.1
  17.4 12.6 %all-to-all-done.1 = bf16[4,256,256]{2,1,0:T(8,128)(2,1)S(1)} async-done(((bf16[4,256,256]{2,1,0:T(8,128)(2,1)}), bf16[4,256,256]{2,1,0:T(8,128)(2,1)S(1)}, u32[]{:S(2)}, u32[]{:S(2)}) %all-to-all-start.1) | async-done | bytes 524320 | tf_op jit(solution)/shard_map/all_to_all | solution.py:54
  30.0 3.5 all-to-all-start
  33.5 4.8 copy.498
  38.2 9.2 %all-to-all-done = bf16[256,4,256]{2,0,1:T(8,128)(2,1)S(1)} async-done(((bf16[256,4,256]{2,0,1:T(8,128)(2,1)}), bf16[256,4,256]{2,0,1:T(8,128)(2,1)S(1)}, u32[]{:S(2)}, u32[]{:S(2)}) %all-to-all-start) | async-done | bytes 524320 | tf_op jit(solution)/shard_map/all_to_all | solution.py:59
  47.4 5.0 all-to-all-start.2
  53.1 4.7 copy.497
  58.9 3.4 collective-permute-start
  62.3 2.1 collective-permute-start.1
  64.4 4.0 collective-permute-start.2
  68.4 4.0 collective-permute-start.3
  78.5 7.6 %collective-permute-done.2 = bf16[1024,256]{1,0:T(8,128)(2,1)} collective-permute-done((bf16[1024,256]{1,0:T(8,128)(2,1)S(1)}, bf16[1024,256]{1,0:T(8,128)(2,1)}, u32[]{:S(2)}, u32[]{:S(2)}) %collective-permute-start.2) | collective-permute-done | bytes 524320 | tf_op jit(solution)/shard_map/ppermute | solution.py:16
  93.1 52.1 %all-to-all-done.2 = bf16[256,4,2048]{2,0,1:T(8,128)(2,1)} async-done(((bf16[256,4,2048]{2,0,1:T(8,128)(2,1)}), bf16[256,4,2048]{2,0,1:T(8,128)(2,1)}, u32[]{:S(2)}, u32[]{:S(2)}) %all-to-all-start.2) | async-done | bytes 4194336 | tf_op jit(solution)/shard_map/all_to_all | solution.py:52
  145.1 4.8 all-to-all-start.4
  150.0 5.7 copy.377
  155.7 8.5 %bitcast_reduce_fusion = (f32[16,2,8,64]{3,2,1,0:T(8,128)}, f32[16,2,128,64,8]{2,3,4,1,0:T(8,128)}) fusion(pred[16,128]{1,0:T(8,128)(4,1)S(1)} %broadcast_in_dim_reshape.2, bf16[16,64,2,8,128]{4,3,2,1,0:T(8,128)(2,1)} %bitcast.91, bf16[16,128,2,128,1]{3,2,1,0,4:T(2,128)(2,1)S(1)} %bitcast.264), kind=kOutput, calls=%fused_computation.20 | convolution fusion | flops 543145984 | bytes 13699072 | tf_op jit(solution)/shard_map/bqkgd,bskd->bkgqs/dot_general | solution.py:29
  164.2 6.4 fusion.15
  170.7 2.9 select_reduce_fusion.1
  173.6 6.1 fusion.16
  179.7 2.9 select_reduce_fusion
  182.6 4.7 fusion.11
  187.5 4.2 select_convert_fusion
  191.8 5.5 fusion.127
  197.3 5.1 fusion.14
  202.4 4.6 fusion.31
  207.0 9.6 %fusion.8 = bf16[16,64,2,8,128]{4,1,3,0,2:T(8,128)(2,1)} fusion(f32[16,2,128,8,64]{2,4,3,0,1:T(8,128)} %fusion.31, f32[2,128,16,8,64]{1,4,3,2,0:T(8,128)} %fusion.127, bf16[16,2,8,64,64]{3,4,2,0,1:T(8,128)(2,1)S(1)} %get-tuple-element.59, bf16[16,64,2,128,1]{3,2,1,0,4:T(2,128)(2,1)S(1)} %bitcast.256), kind=kOutput, calls=%fused_computation.16 | convolution fusion | flops 274726912 | bytes 23592960 | tf_op jit(solution)/shard_map/bkgqs,bskd->bqkgd/dot_general | solution.py:39
  216.6 26.0 %all-to-all-done.4 = bf16[256,4,2048]{2,0,1:T(8,128)(2,1)} async-done(((bf16[256,4,2048]{2,0,1:T(8,128)(2,1)}), bf16[256,4,2048]{2,0,1:T(8,128)(2,1)}, u32[]{:S(2)}, u32[]{:S(2)}) %all-to-all-start.4) | async-done | bytes 4194336 | tf_op jit(solution)/shard_map/all_to_all | solution.py:147
  242.6 3.7 copy.378
  246.4 3.3 fusion.53
  250.9 2.4 multiply_reduce_fusion
  253.3 6.7 %fusion.3 = bf16[16,2,8,64,128]{4,3,2,1,0:T(8,128)(2,1)} fusion(bf16[16,2,8,64,128]{4,3,2,1,0:T(8,128)(2,1)} %copy-done.6, bf16[16,64,2,8,128]{4,3,2,1,0:T(8,128)(2,1)S(1)} %bitcast.232, bf16[16,128,2,128,1]{3,2,1,0,4:T(2,128)(2,1)S(1)} %bitcast.244, f32[16,64,2,8]{1,3,0,2:T(8,128)S(1)} %multiply_reduce_fusion), kind=kOutput, calls=%fused_computation.7 | convolution fusion | flops 545259520 | bytes 13697024 | tf_op jit(solution)/shard_map/bqkgd,bskd->bkgqs/dot_general | solution.py:29
  260.0 7.8 %fusion.5 = bf16[16,2,8,64,64]{3,4,2,0,1:T(8,128)(2,1)} fusion(bf16[16,2,8,64,64]{3,4,2,0,1:T(8,128)(2,1)} %copy-done.3, f32[16,2,8,64]{3,2,0,1:T(8,128)S(1)} %bitcast.266, bf16[16,64,2,8,128]{4,3,2,1,0:T(8,128)(2,1)S(1)} %bitcast.233, bf16[16,64,2,128,1]{3,2,1,0,4:T(2,128)(2,1)S(1)} %bitcast.257), kind=kOutput, calls=%fused_computation.11 | convolution fusion | flops 272629760 | bytes 8978432 | tf_op jit(solution)/shard_map/bqkgd,bskd->bkgqs/dot_general | solution.py:29
  267.8 5.6 fusion.7
  273.5 2.6 fusion.61
  276.1 4.2 fusion.50
  281.9 2.7 reshape.252
  284.6 3.2 copy.315
  287.8 2.8 reshape.253
  290.7 5.1 fusion.136
  297.9 2.4 slice.87
  306.1 6.1 fusion.71
  314.8 5.1 fusion.91
  322.3 5.1 fusion.81
  327.5 3.1 copy.311
  332.1 3.0 copy.322
  337.2 13.5 %collective-permute-done.7 = bf16[1024,256]{1,0:T(8,128)(2,1)} collective-permute-done((bf16[1024,256]{1,0:T(8,128)(2,1)}, bf16[1024,256]{1,0:T(8,128)(2,1)}, u32[]{:S(2)}, u32[]{:S(2)}) %collective-permute-start.7) | collective-permute-done | bytes 524320 | tf_op jit(solution)/shard_map/ppermute | solution.py:16
  352.4 40.7 %all-reduce.5.cloned.1.call-done = (f32[64,256]{1,0:T(8,128)}, f32[64,256]{1,0:T(8,128)}) async-done(((f32[64,256]{1,0:T(8,128)}, f32[64,256]{1,0:T(8,128)}), (f32[64,256]{1,0:T(8,128)}, f32[64,256]{1,0:T(8,128)})) %all-reduce.5.cloned.1.call-update) | async-done | bytes 131088 | tf_op jit(solution)/shard_map/psum | solution.py:167
  394.9 4.6 all-to-all-start.6
  399.5 7.4 %fusion.129 = f32[2,128,16,8,64]{1,4,3,2,0:T(8,128)} fusion(bf16[16,2,8,64,64]{3,4,2,0,1:T(8,128)(2,1)} %fusion.7, bf16[64,2,128]{2,0,1:T(8,128)(2,1)S(1)} %copy-done.28), kind=kOutput, calls=%fused_computation.144 | convolution fusion | flops 268435456 | bytes 10518528 | tf_op jit(solution)/shard_map/bkgqs,skd->bqkgd/dot_general | solution.py:36
  406.9 4.5 fusion.29
  412.3 5.2 all-to-all-start.7
  417.5 9.0 %fusion.1 = bf16[16,64,2,8,128]{4,1,3,0,2:T(8,128)(2,1)S(1)} fusion(f32[16,2,128,8,64]{2,4,3,0,1:T(8,128)} %fusion.29, f32[2,128,16,8,64]{1,4,3,2,0:T(8,128)} %fusion.129, bf16[16,2,8,64,64]{3,4,2,0,1:T(8,128)(2,1)} %fusion.5, bf16[16,64,2,128,1]{3,2,1,0,4:T(2,128)(2,1)S(1)} %bitcast.255), kind=kOutput, calls=%fused_computation.4 | convolution fusion | flops 276824064 | bytes 23592960 | tf_op jit(solution)/shard_map/bkgqs,bskd->bqkgd/dot_general | solution.py:39
  426.6 5.6 copy.307
  432.2 7.3 %all_to_all.112 = bf16[4,256,2048]{2,1,0:T(8,128)(2,1)} reshape(bf16[16,64,2,8,128]{4,3,2,1,0:T(8,128)(2,1)} %copy.307) | data formatting | bytes 8388608 | tf_op jit(solution)/shard_map/all_to_all | solution.py:212
  439.5 5.1 all-to-all-start.5
  444.6 7.7 %copy.292 = bf16[16,64,2,8,128]{4,3,2,1,0:T(8,128)(2,1)} copy(bf16[16,64,2,8,128]{4,1,3,0,2:T(8,128)(2,1)} %fusion.8) | data formatting | bytes 8388608 | tf_op jit(solution)/shard_map/optimization_barrier | solution.py:143
  452.3 7.3 %all_to_all.105 = bf16[4,256,2048]{2,1,0:T(8,128)(2,1)} reshape(bf16[16,64,2,8,128]{4,3,2,1,0:T(8,128)(2,1)} %copy.292) | data formatting | bytes 8388608 | tf_op jit(solution)/shard_map/all_to_all | solution.py:144
  459.6 75.8 %all-to-all-done.5 = bf16[4,256,2048]{2,1,0:T(8,128)(2,1)} async-done(((bf16[4,256,2048]{2,1,0:T(8,128)(2,1)}), bf16[4,256,2048]{2,1,0:T(8,128)(2,1)}, u32[]{:S(2)}, u32[]{:S(2)}) %all-to-all-start.5) | async-done | bytes 4194336 | tf_op jit(solution)/shard_map/all_to_all | solution.py:212
  535.4 4.9 all-to-all-start.3
  542.0 6.2 copy.308
  548.2 6.3 copy.328
  554.5 78.4 %all-to-all-done.3 = bf16[4,256,2048]{2,1,0:T(8,128)(2,1)} async-done(((bf16[4,256,2048]{2,1,0:T(8,128)(2,1)}), bf16[4,256,2048]{2,1,0:T(8,128)(2,1)}, u32[]{:S(2)}, u32[]{:S(2)}) %all-to-all-start.3) | async-done | bytes 4194336 | tf_op jit(solution)/shard_map/all_to_all | solution.py:144
  632.9 6.2 copy.293
  639.1 6.3 copy.327
  (131 shorter events, 44.2 us)
Async XLA Ops:
  9.2 20.8 %all-to-all-start.1 = ((bf16[4,256,256]{2,1,0:T(8,128)(2,1)}), bf16[4,256,256]{2,1,0:T(8,128)(2,1)S(1)}, u32[]{:S(2)}, u32[]{:S(2)}) async-start(bf16[4,256,256]{2,1,0:T(8,128)(2,1)} %pad_maximum_fusion.2), calls=%async_computation.1 | async-start | bytes 1048576 | tf_op jit(solution)/shard_map/all_to_all | solution.py:54
  30.0 17.4 %all-to-all-start = ((bf16[256,4,256]{2,0,1:T(8,128)(2,1)}), bf16[256,4,256]{2,0,1:T(8,128)(2,1)S(1)}, u32[]{:S(2)}, u32[]{:S(2)}) async-start(bf16[256,4,256]{2,0,1:T(8,128)(2,1)} %bitcast.227), calls=%async_computation | async-start | bytes 1048576 | tf_op jit(solution)/shard_map/all_to_all | solution.py:59
  47.4 5.1 copy-start.30
  47.4 97.7 %all-to-all-start.2 = ((bf16[256,4,2048]{2,0,1:T(8,128)(2,1)}), bf16[256,4,2048]{2,0,1:T(8,128)(2,1)}, u32[]{:S(2)}, u32[]{:S(2)}) async-start(bf16[256,4,2048]{2,0,1:T(8,128)(2,1)} %bitcast.240), calls=%async_computation.2 | async-start | bytes 8388608 | tf_op jit(solution)/shard_map/all_to_all | solution.py:52
  52.4 111.8 %all-reduce.7.cloned.1.call-start = ((), (), s32[]{:S(2)}) async-start(), calls=%async_computation.9 | async-start | bytes 131072 | tf_op jit(solution)/shard_map/psum | solution.py:21
  58.9 111.8 %copy-start.23 = (pred[16,64,64]{1,2,0:T(8,128)(4,1)}, pred[16,64,64]{1,2,0:T(8,128)(4,1)S(1)}, u32[]{:S(2)}) copy-start(pred[16,64,64]{1,2,0:T(8,128)(4,1)S(1)} %get-tuple-element.62) | copy-start | bytes 196612
  58.9 15.9 %collective-permute-start = (bf16[1024,256]{1,0:T(8,128)(2,1)S(1)}, bf16[1024,256]{1,0:T(8,128)(2,1)S(1)}, u32[]{:S(2)}, u32[]{:S(2)}) collective-permute-start(bf16[1024,256]{1,0:T(8,128)(2,1)S(1)} %bitcast.250), channel_id=1, source_target_pairs={{0,8},{4,12},{8,16},{12,20},{16,24},{20,28},{1,9},{5,13},{9,17},{1... | collective-permute-start | bytes 1572872 | tf_op jit(solution)/shard_map/ppermute | solution.py:16
  62.3 13.3 %collective-permute-start.1 = (bf16[1024,256]{1,0:T(8,128)(2,1)S(1)}, bf16[1024,256]{1,0:T(8,128)(2,1)}, u32[]{:S(2)}, u32[]{:S(2)}) collective-permute-start(bf16[1024,256]{1,0:T(8,128)(2,1)S(1)} %bitcast.251), channel_id=1, source_target_pairs={{0,4},{4,8},{8,12},{12,16},{16,20},{20,24},{24,28},{1,5},{5,9},{9,... | collective-permute-start | bytes 1572872 | tf_op jit(solution)/shard_map/ppermute | solution.py:16
  64.4 21.7 %collective-permute-start.2 = (bf16[1024,256]{1,0:T(8,128)(2,1)S(1)}, bf16[1024,256]{1,0:T(8,128)(2,1)}, u32[]{:S(2)}, u32[]{:S(2)}) collective-permute-start(bf16[1024,256]{1,0:T(8,128)(2,1)S(1)} %bitcast.245), channel_id=1, source_target_pairs={{0,8},{4,12},{8,16},{12,20},{16,24},{20,28},{1,9},{5,13},{9,17},{1... | collective-permute-start | bytes 1572872 | tf_op jit(solution)/shard_map/ppermute | solution.py:16
  68.4 17.7 %collective-permute-start.3 = (bf16[1024,256]{1,0:T(8,128)(2,1)S(1)}, bf16[1024,256]{1,0:T(8,128)(2,1)}, u32[]{:S(2)}, u32[]{:S(2)}) collective-permute-start(bf16[1024,256]{1,0:T(8,128)(2,1)S(1)} %bitcast.246), channel_id=1, source_target_pairs={{0,4},{4,8},{8,12},{12,16},{16,20},{20,24},{24,28},{1,5},{5,9},{9,... | collective-permute-start | bytes 1572872 | tf_op jit(solution)/shard_map/ppermute | solution.py:16
  74.7 98.8 %copy-start.12 = (bf16[16,64,2,128]{3,2,1,0:T(2,128)(2,1)}, bf16[16,64,2,128]{3,2,1,0:T(2,128)(2,1)S(1)}, u32[]{:S(2)}) copy-start(bf16[16,64,2,128]{3,2,1,0:T(2,128)(2,1)S(1)} %reshape_reshape.3) | copy-start | bytes 1572868
  74.8 0.9 copy-start.27
  145.1 97.5 %all-to-all-start.4 = ((bf16[256,4,2048]{2,0,1:T(8,128)(2,1)}), bf16[256,4,2048]{2,0,1:T(8,128)(2,1)}, u32[]{:S(2)}, u32[]{:S(2)}) async-start(bf16[256,4,2048]{2,0,1:T(8,128)(2,1)} %bitcast.239), calls=%async_computation.4 | async-start | bytes 8388608 | tf_op jit(solution)/shard_map/all_to_all | solution.py:147
  150.0 243.2 %all-reduce.5.cloned.1.call-start = ((), (), s32[]{:S(2)}) async-start(), calls=%async_computation.8 | async-start | bytes 262144 | tf_op jit(solution)/shard_map/psum | solution.py:167
  150.0 5.7 copy-start.16
  170.6 2.9 copy-start.21
  170.7 11.9 %slice-start = ((s8[8388608]{0:T(1024)(128)(4,1)}), s8[4194304]{0:T(1024)(128)(4,1)S(1)}, s32[]{:S(2)}) async-start(s8[8388608]{0:T(1024)(128)(4,1)} %bitcast.237), calls=%async_computation.10 | async-start | bytes 8388608
  173.5 9.0 %slice-start.1 = ((s8[8388608]{0:T(1024)(128)(4,1)}), s8[4194304]{0:T(1024)(128)(4,1)S(1)}, s32[]{:S(2)}) async-start(s8[8388608]{0:T(1024)(128)(4,1)} %bitcast.237), calls=%async_computation.11 | async-start | bytes 8388608
  179.7 2.9 copy-start.26
  182.6 4.9 copy-start.22
  182.6 4.9 copy-start.24
  187.5 4.3 copy-start.29
  191.8 5.5 copy-start.1
  191.8 15.2 %copy-start.3 = (bf16[16,2,8,64,64]{3,4,2,0,1:T(8,128)(2,1)}, bf16[16,2,8,64,64]{3,4,2,0,1:T(8,128)(2,1)S(1)}, u32[]{:S(2)}) copy-start(bf16[16,2,8,64,64]{3,4,2,0,1:T(8,128)(2,1)S(1)} %get-tuple-element.59) | copy-start | bytes 6291460
  197.3 5.1 copy-start.10
  202.4 4.6 copy-start.6
  202.4 4.6 copy-start.14
  242.6 3.8 copy-start.7
  246.4 27.1 %copy-start = (bf16[128,8,16,128]{3,2,1,0:T(8,128)(2,1)}, bf16[128,8,16,128]{3,2,1,0:T(8,128)(2,1)S(1)}, u32[]{:S(2)}) copy-start(bf16[128,8,16,128]{3,2,1,0:T(8,128)(2,1)S(1)} %copy.378) | copy-start | bytes 12582916
  246.4 4.5 copy-start.5
  250.9 2.4 copy-start.11
  260.0 7.8 %copy-start.2 = (bf16[16,2,8,64,64]{3,4,2,0,1:T(8,128)(2,1)S(1)}, bf16[16,2,8,64,64]{3,4,2,0,1:T(8,128)(2,1)}, u32[]{:S(2)}) copy-start(bf16[16,2,8,64,64]{3,4,2,0,1:T(8,128)(2,1)} %copy-done.1) | copy-start | bytes 6291460
  267.8 5.6 copy-start.4
  273.4 2.6 copy-start.8
  300.3 34.9 %collective-permute-start.4 = (f32[1024,256]{1,0:T(8,128)}, f32[1024,256]{1,0:T(8,128)}, u32[]{:S(2)}, u32[]{:S(2)}) collective-permute-start(f32[1024,256]{1,0:T(8,128)} %slice.87), channel_id=1, source_target_pairs={{4,0},{8,4},{12,8},{16,12},{20,16},{24,20},{28,24},{5,1},{9,5},{13... | collective-permute-start | bytes 3145736 | tf_op jit(solution)/shard_map/ppermute | solution.py:16
  304.7 7.5 %copy-start.20 = (f32[16,16384]{1,0:T(8,128)S(1)}, f32[16,16384]{1,0:T(8,128)}, u32[]{:S(2)}) copy-start(f32[16,16384]{1,0:T(8,128)} %get-tuple-element.49) | copy-start | bytes 3145732
  304.7 30.5 %collective-permute-start.5 = (bf16[1024,256]{1,0:T(8,128)(2,1)}, bf16[1024,256]{1,0:T(8,128)(2,1)}, u32[]{:S(2)}, u32[]{:S(2)}) collective-permute-start(bf16[1024,256]{1,0:T(8,128)(2,1)} %convert_element_type.73), channel_id=1, source_target_pairs={{8,0},{12,4},{16,8},{20,12},{24,16},{28,20},{9,1},{13,5},{17,9},{2... | collective-permute-start | bytes 1572872 | tf_op jit(solution)/shard_map/ppermute | solution.py:16
  313.3 6.5 copy-start.25
  313.3 37.4 %collective-permute-start.6 = (f32[1024,256]{1,0:T(8,128)}, f32[1024,256]{1,0:T(8,128)}, u32[]{:S(2)}, u32[]{:S(2)}) collective-permute-start(f32[1024,256]{1,0:T(8,128)} %slice.92), channel_id=1, source_target_pairs={{4,0},{8,4},{12,8},{16,12},{20,16},{24,20},{28,24},{5,1},{9,5},{13... | collective-permute-start | bytes 3145736 | tf_op jit(solution)/shard_map/ppermute | solution.py:16
  320.9 6.5 copy-start.19
  320.9 29.8 %collective-permute-start.7 = (bf16[1024,256]{1,0:T(8,128)(2,1)}, bf16[1024,256]{1,0:T(8,128)(2,1)}, u32[]{:S(2)}, u32[]{:S(2)}) collective-permute-start(bf16[1024,256]{1,0:T(8,128)(2,1)} %convert_element_type.76), channel_id=1, source_target_pairs={{8,0},{12,4},{16,8},{20,12},{24,16},{28,20},{9,1},{13,5},{17,9},{2... | collective-permute-start | bytes 1572872 | tf_op jit(solution)/shard_map/ppermute | solution.py:16
  327.3 4.6 copy-start.18
  335.1 15.6 %copy-start.15 = (f32[16,64,2,128]{3,2,1,0:T(2,128)S(1)}, f32[16,64,2,128]{3,2,1,0:T(2,128)}, u32[]{:S(2)}) copy-start(f32[16,64,2,128]{3,2,1,0:T(2,128)} %copy.322) | copy-start | bytes 3145732
  337.2 62.3 %copy-start.28 = (bf16[64,2,128]{2,0,1:T(8,128)(2,1)S(1)}, bf16[64,2,128]{2,0,1:T(8,128)(2,1)}, u32[]{:S(2)}) copy-start(bf16[64,2,128]{2,0,1:T(8,128)(2,1)} %get-tuple-element.47) | copy-start | bytes 98308
  394.9 17.5 %all-to-all-start.6 = ((bf16[4,256,256]{2,1,0:T(8,128)(2,1)}), bf16[4,256,256]{2,1,0:T(8,128)(2,1)S(1)}, u32[]{:S(2)}, u32[]{:S(2)}) async-start(bf16[4,256,256]{2,1,0:T(8,128)(2,1)} %bitcast.55), calls=%async_computation.6 | async-start | bytes 1048576 | tf_op jit(solution)/shard_map/all_to_all | solution.py:213
  399.5 7.4 %copy-start.9 = (bf16[16,2,8,64,128]{4,3,2,1,0:T(8,128)(2,1)S(1)}, bf16[16,2,8,64,128]{4,3,2,1,0:T(8,128)(2,1)}, u32[]{:S(2)}) copy-start(bf16[16,2,8,64,128]{4,3,2,1,0:T(8,128)(2,1)} %fusion.3) | copy-start | bytes 12582916
  399.5 7.4 %copy-start.17 = (bf16[16,128,2,128]{3,2,1,0:T(2,128)(2,1)S(1)}, bf16[16,128,2,128]{3,2,1,0:T(2,128)(2,1)}, u32[]{:S(2)}) copy-start(bf16[16,128,2,128]{3,2,1,0:T(2,128)(2,1)} %reshape.246) | copy-start | bytes 3145732
  406.9 10.7 %copy-start.13 = (bf16[16,64,2,128]{3,2,1,0:T(2,128)(2,1)S(1)}, bf16[16,64,2,128]{3,2,1,0:T(2,128)(2,1)}, u32[]{:S(2)}) copy-start(bf16[16,64,2,128]{3,2,1,0:T(2,128)(2,1)} %copy-done.12) | copy-start | bytes 1572868
  412.3 27.1 %all-to-all-start.7 = ((bf16[4,256,256]{2,1,0:T(8,128)(2,1)}), bf16[4,256,256]{2,1,0:T(8,128)(2,1)S(1)}, u32[]{:S(2)}, u32[]{:S(2)}) async-start(bf16[4,256,256]{2,1,0:T(8,128)(2,1)} %bitcast.63), calls=%async_computation.7 | async-start | bytes 1048576 | tf_op jit(solution)/shard_map/all_to_all | solution.py:216
  439.5 95.9 %all-to-all-start.5 = ((bf16[4,256,2048]{2,1,0:T(8,128)(2,1)}), bf16[4,256,2048]{2,1,0:T(8,128)(2,1)}, u32[]{:S(2)}, u32[]{:S(2)}) async-start(bf16[4,256,2048]{2,1,0:T(8,128)(2,1)} %all_to_all.112), calls=%async_computation.5 | async-start | bytes 8388608 | tf_op jit(solution)/shard_map/all_to_all | solution.py:212
  535.4 97.5 %all-to-all-start.3 = ((bf16[4,256,2048]{2,1,0:T(8,128)(2,1)}), bf16[4,256,2048]{2,1,0:T(8,128)(2,1)}, u32[]{:S(2)}, u32[]{:S(2)}) async-start(bf16[4,256,2048]{2,1,0:T(8,128)(2,1)} %all_to_all.105), calls=%async_computation.3 | async-start | bytes 8388608 | tf_op jit(solution)/shard_map/all_to_all | solution.py:144
Sparse Core Ops, SparseCore 0:
  74.7 52.4 all-reduce.6
  335.3 57.8 all-reduce.4
